TPU v7x, 32 devices: a whole 2x2x4 slice. The times are simulated.
32 devices in a mesh: section: 4 (over y, core), row: 2 (over x), col: 4 (over z).
Axes of the slice: x: 2, y: 2, z: 4, core: 2. Of those that a mesh axis runs over, the one named last changes fastest.
Arguments:
- incoming: bfloat16 [4, 128, 12288], P('section', 'col', 'row'), may hold values from -6 to 6
- loss_grad: bfloat16 [128, 12288], P('col', 'row'), may hold values from -6 to 6
- out_proj_t: bfloat16 [4, 12288, 6144], P('section', 'row', 'col'), may hold values from -0.0546875 to 0.0546875
- query_proj_t: bfloat16 [4, 6144, 12288], P('section', 'col', 'row'), may hold values from -0.078125 to 0.078125
- saved_query: bfloat16 [2, 4, 128, 6144], P(None, 'section', None, 'col'), may hold values from -43 to 43
- saved_key: bfloat16 [2, 4, 128, 6144], P(None, 'section', None, 'col'), may hold values from -4 to 4
- saved_value: bfloat16 [2, 4, 128, 6144], P(None, 'section', None, 'col'), may hold values from -48 to 48
- pattern: int32 [48, 2, 3], replicated, may hold values from 0 to 1, as said below
- plan: int32 [4, 2], replicated, may hold values from 0 to 1, as said below
Outputs:
- handed_first: bfloat16 [4, 128, 12288], P('section', 'col', 'row')
- handed_second: bfloat16 [4, 128, 12288], P('section', 'col', 'row')
Inputs may be any that keep to these rules, and one draw needn't show every extreme that they name: pattern[h, i, 0] = i, and every entry of pattern[h, i, :] lies between 0 and i. plan[s, 1] = (plan[s, 0] + 1) % 2.
All inputs are finite; a program needn't handle non-finite values.
Results may differ from a plain program's by a relative error of at most 0.012.
Values may be sent and summed in bfloat16 or wider, within the bound.
No kernel may reach another device: no remote copies, remote signals or barrier semaphores. Data moves between devices by JAX's collectives and lax.ppermute only.
A program may use at most 128 MiB of HBM per device.

v0:
```python
import jax
import jax.numpy as jnp
from jax import lax
from jax.sharding import PartitionSpec as P

HD = 128
BLOCK = 64


def shifted(block, axis, distance):
    devices = range(lax.axis_size(axis))
    route = [(i - distance, i) for i in devices if i - distance in devices]
    return lax.ppermute(block, axis, route)


def token_mask(pattern_part, tokens):
    blocks = tokens // BLOCK
    member = jnp.any(
        pattern_part[:, :, :, None] == jnp.arange(blocks, dtype=jnp.int32)[None, None, None, :],
        axis=2,
    )
    member = jnp.repeat(jnp.repeat(member, BLOCK, axis=1), BLOCK, axis=2)
    positions = jnp.arange(tokens, dtype=jnp.int32)
    return member & (positions[:, None] >= positions[None, :])[None]


def attend_rows(upstream, query_rows, key_rows, value_rows, allowed):
    row_count = query_rows.shape[0]
    head_count = query_rows.shape[1] // HD
    inverse_root = HD ** (-0.5)
    q_heads = query_rows.reshape(row_count, head_count, HD)
    k_heads = key_rows.reshape(key_rows.shape[0], head_count, HD)
    v_heads = value_rows.reshape(value_rows.shape[0], head_count, HD)
    up_heads = upstream.reshape(row_count, head_count, HD)
    scores = (
        jnp.einsum("thd,uhd->htu", q_heads, k_heads, preferred_element_type=jnp.float32)
        * inverse_root
    )
    masked = jnp.where(allowed, scores, -jnp.inf)
    row_peak = jnp.max(masked, axis=-1, keepdims=True)
    exp_terms = jnp.where(allowed, jnp.exp(masked - row_peak), 0.0)
    row_total = jnp.sum(exp_terms, axis=-1, keepdims=True)
    prob_rows = exp_terms / row_total
    prob_grad = jnp.einsum("thd,uhd->htu", up_heads, v_heads, preferred_element_type=jnp.float32)
    row_delta = jnp.sum(prob_rows * prob_grad, axis=-1, keepdims=True)
    dscore = (prob_rows * (prob_grad - row_delta)).astype(jnp.bfloat16)
    dquery = (
        jnp.einsum("htu,uhd->thd", dscore, k_heads, preferred_element_type=jnp.float32)
        * inverse_root
    )
    return dquery.reshape(row_count, head_count * HD).astype(jnp.bfloat16)


def body(
    incoming,
    loss_grad,
    out_proj_t,
    query_proj_t,
    saved_query,
    saved_key,
    saved_value,
    pattern,
    plan,
):
    section_at = lax.axis_index("section")
    section_count = lax.axis_size("section")
    col_at = lax.axis_index("col")
    w_out = out_proj_t[0]
    w_query = query_proj_t[0]
    head_count = w_out.shape[1] // HD
    tokens = saved_query.shape[2]
    local_pattern = lax.dynamic_slice_in_dim(pattern, col_at * head_count, head_count, 0)
    allowed = token_mask(local_pattern, tokens)

    def section_step(gradient, turn_index):
        slot_index = lax.dynamic_index_in_dim(plan[:, turn_index], section_at, 0, keepdims=False)
        query_rows = lax.dynamic_index_in_dim(saved_query[:, 0], slot_index, 0, keepdims=False)
        key_rows = lax.dynamic_index_in_dim(saved_key[:, 0], slot_index, 0, keepdims=False)
        value_rows = lax.dynamic_index_in_dim(saved_value[:, 0], slot_index, 0, keepdims=False)
        gathered = lax.all_gather(gradient, "col", axis=0, tiled=True)
        partial_value = jnp.dot(gathered, w_out, preferred_element_type=jnp.float32)
        upstream = lax.psum(partial_value, "row").astype(jnp.bfloat16)
        dquery = attend_rows(upstream, query_rows, key_rows, value_rows, allowed)
        mixed_back = lax.psum_scatter(
            jnp.dot(dquery, w_query, preferred_element_type=jnp.float32),
            "col",
            scatter_dimension=0,
            tiled=True,
        )
        return (gradient.astype(jnp.float32) + mixed_back).astype(jnp.bfloat16)

    handed_first = section_step(incoming[0], 0)
    received = shifted(handed_first, "section", -1)
    second_input = jnp.where(section_at == section_count - 1, loss_grad, received)
    handed_second = section_step(second_input, 1)
    return (handed_first[None], handed_second[None])


def solution(mesh):
    return jax.shard_map(
        body,
        mesh=mesh,
        in_specs=(
            P("section", "col", "row"),
            P("col", "row"),
            P("section", "row", "col"),
            P("section", "col", "row"),
            P(None, "section", None, "col"),
            P(None, "section", None, "col"),
            P(None, "section", None, "col"),
            P(),
            P(),
        ),
        out_specs=(P("section", "col", "row"), P("section", "col", "row")),
        check_vma=False,
    )
```

profile of v0, /device:TPU:0, one launch (start us, length us, event | category | flops | bytes accessed | tf_op | source)
XLA Modules:
  0.0 316.1 jit_solution(6484015701918346007)
XLA Ops:
  13.2 1.2 constant_dynamic-slice_fusion.2
  15.0 1.2 constant_dynamic-slice_fusion.1
  16.4 1.2 constant_dynamic-slice_fusion
  18.0 1.4 fusion.35
  19.4 1.2 fusion.17
  20.6 28.7 %all-gather.6.cloned.1.call-done = bf16[1,128,6144]{2,1,0:T(8,128)(2,1)} async-done(((bf16[1,32,6144]{2,1,0:T(8,128)(2,1)}), bf16[1,128,6144]{2,1,0:T(8,128)(2,1)}) %all-gather.6.cloned.1.call-update) | async-done | bytes 1572880 | tf_op jit(solution)/shard_map/all_gather | solution.py:80
  49.3 8.2 %fusion.8 = f32[128,1536]{1,0:T(8,128)S(1)} fusion(bf16[1,6144,1536]{2,1,0:T(8,128)(2,1)} %param.11, bf16[1,128,6144]{2,1,0:T(8,128)(2,1)} %all-gather.6.cloned.1.call-done), kind=kOutput, calls=%fused_computation.8 | convolution fusion | flops 2415919104 | bytes 21233664 | tf_op jit(solution)/shard_map/dot_general | solution.py:81
  57.6 21.3 %all-reduce.2 = bf16[128,1536]{1,0:T(8,128)(2,1)S(1)} all-reduce(f32[128,1536]{1,0:T(8,128)S(1)} %fusion.8), channel_id=1, replica_groups=mesh['section'=4,'row'=2,'col'=4] {'row'}, use_global_device_ids=true, to_apply=%region_3.4 | all-reduce | flops 196608 | bytes 1179648 | tf_op jit(solution)/shard_map/psum | solution.py:82
  79.1 2.4 multiply_reduce_fusion.1
  81.5 2.2 fusion.22
  83.9 10.8 %fusion.4 = f32[128,6144]{1,0:T(8,128)} fusion(bf16[128,1536]{0,1:T(8,128)(2,1)S(1)} %bitcast.58, bf16[1,1536,6144]{2,1,0:T(8,128)(2,1)} %param.12), kind=kOutput, calls=%fused_computation.4 | convolution fusion | flops 2415919104 | bytes 22413312 | tf_op jit(solution)/shard_map/dot_general | solution.py:85
  94.8 60.4 %reduce-scatter.3.cloned.1.call-done = f32[32,6144]{1,0:T(8,128)} async-done(((f32[128,6144]{1,0:T(8,128)}), f32[32,6144]{1,0:T(8,128)}) %reduce-scatter.3.cloned.1.call-update) | async-done | bytes 786448 | tf_op jit(solution)/shard_map/reduce_scatter | solution.py:84
  155.2 1.2 fusion.23
  156.4 1.3 collective-permute-start
  157.7 2.3 collective-permute-done
  161.6 1.4 fusion.36
  163.4 38.7 %all-gather.4.cloned.1.call-done = bf16[128,6144]{1,0:T(8,128)(2,1)} async-done(((bf16[32,6144]{1,0:T(8,128)(2,1)}), bf16[128,6144]{1,0:T(8,128)(2,1)}) %all-gather.4.cloned.1.call-update) | async-done | bytes 1572880 | tf_op jit(solution)/shard_map/all_gather | solution.py:80
  202.0 8.2 %fusion.6 = f32[128,1536]{1,0:T(8,128)S(1)} fusion(bf16[128,6144]{1,0:T(8,128)(2,1)} %all-gather.4.cloned.1.call-done, bf16[1,6144,1536]{2,1,0:T(8,128)(2,1)} %param.11), kind=kOutput, calls=%fused_computation.6 | convolution fusion | flops 2415919104 | bytes 21233664 | tf_op jit(solution)/shard_map/dot_general | solution.py:81
  210.2 21.4 %all-reduce.3 = bf16[128,1536]{1,0:T(8,128)(2,1)S(1)} all-reduce(f32[128,1536]{1,0:T(8,128)S(1)} %fusion.6), channel_id=1, replica_groups=mesh['section'=4,'row'=2,'col'=4] {'row'}, use_global_device_ids=true, to_apply=%region_8.9 | all-reduce | flops 196608 | bytes 1179648 | tf_op jit(solution)/shard_map/psum | solution.py:82
  231.9 2.4 multiply_reduce_fusion
  234.3 1.7 fusion.21
  236.3 10.8 %fusion.2 = f32[128,6144]{1,0:T(8,128)} fusion(bf16[128,1536]{0,1:T(8,128)(2,1)S(1)} %bitcast.59, bf16[1,1536,6144]{2,1,0:T(8,128)(2,1)} %param.12), kind=kOutput, calls=%fused_computation.2 | convolution fusion | flops 2415919104 | bytes 22413312 | tf_op jit(solution)/shard_map/dot_general | solution.py:85
  247.1 60.5 %reduce-scatter.5.cloned.1.call-done = f32[32,6144]{1,0:T(8,128)} async-done(((f32[128,6144]{1,0:T(8,128)}), f32[32,6144]{1,0:T(8,128)}) %reduce-scatter.5.cloned.1.call-update) | async-done | bytes 786448 | tf_op jit(solution)/shard_map/reduce_scatter | solution.py:84
  307.6 2.0 fusion.24
  (43 shorter events, 6.2 us)
Async XLA Ops:
  7.2 7.4 %copy-start = (s32[48,2,3]{0,1,2:T(2,128)S(1)}, s32[48,2,3]{0,1,2:T(2,128)}, u32[]{:S(2)}) copy-start(s32[48,2,3]{0,1,2:T(2,128)} %param.16) | copy-start | bytes 3460
  7.2 42.2 %all-gather.6.cloned.1.call-start = ((), (), s32[]{:S(2)}) async-start(), calls=%async_computation.5 | async-start | bytes 1966080 | tf_op jit(solution)/shard_map/all_gather | solution.py:80
  7.9 147.3 %reduce-scatter.3.cloned.1.call-start = ((), (), s32[]{:S(2)}) async-start(), calls=%async_computation.2 | async-start | bytes 3932160 | tf_op jit(solution)/shard_map/reduce_scatter | solution.py:84
  79.1 76.1 %copy-start.3 = (bf16[1,32,6144]{2,1,0:T(8,128)(2,1)S(1)}, bf16[1,32,6144]{2,1,0:T(8,128)(2,1)}, u32[]{:S(2)}) copy-start(bf16[1,32,6144]{2,1,0:T(8,128)(2,1)} %param.9) | copy-start | bytes 1179652
  81.5 78.6 %copy-start.4 = (bf16[32,6144]{1,0:T(8,128)(2,1)S(1)}, bf16[32,6144]{1,0:T(8,128)(2,1)}, u32[]{:S(2)}) copy-start(bf16[32,6144]{1,0:T(8,128)(2,1)} %param.10) | copy-start | bytes 1179652
  94.7 107.3 %all-gather.4.cloned.1.call-start = ((), (), s32[]{:S(2)}) async-start(), calls=%async_computation.3 | async-start | bytes 1966080 | tf_op jit(solution)/shard_map/all_gather | solution.py:80
  156.4 4.7 %copy-start.5 = (bf16[32,6144]{1,0:T(8,128)(2,1)}, bf16[32,6144]{1,0:T(8,128)(2,1)S(1)}, u32[]{:S(2)}) copy-start(bf16[32,6144]{1,0:T(8,128)(2,1)S(1)} %fusion.23) | copy-start | bytes 1179652
  156.4 3.6 %collective-permute-start = (bf16[32,6144]{1,0:T(8,128)(2,1)S(1)}, bf16[32,6144]{1,0:T(8,128)(2,1)S(1)}, u32[]{:S(2)}, u32[]{:S(2)}) collective-permute-start(bf16[32,6144]{1,0:T(8,128)(2,1)S(1)} %fusion.23), channel_id=1, source_target_pairs={{8,0},{16,8},{24,16},{9,1},{17,9},{25,17},{10,2},{18,10},{26,18},{... | collective-permute-start | bytes 1179656 | tf_op jit(solution)/shard_map/ppermute | solution.py:13
  160.9 146.7 %reduce-scatter.5.cloned.1.call-start = ((), (), s32[]{:S(2)}) async-start(), calls=%async_computation.4 | async-start | bytes 3932160 | tf_op jit(solution)/shard_map/reduce_scatter | solution.py:84
  231.9 75.6 %copy-start.2 = (bf16[32,6144]{1,0:T(8,128)(2,1)S(1)}, bf16[32,6144]{1,0:T(8,128)(2,1)}, u32[]{:S(2)}) copy-start(bf16[32,6144]{1,0:T(8,128)(2,1)} %broadcast_select_fusion) | copy-start | bytes 1179652
  231.9 77.6 %copy-start.1 = (s32[48,2,3]{0,1,2:T(2,128)S(1)}, s32[48,2,3]{0,1,2:T(2,128)}, u32[]{:S(2)}) copy-start(s32[48,2,3]{0,1,2:T(2,128)} %param.16) | copy-start | bytes 3460
Sparse Core Ops, SparseCore 0:
  9.6 39.7 all-gather.5
  94.8 60.3 reduce-scatter.2
  161.0 40.9 all-gather.3
  247.2 60.3 reduce-scatter.4
where the time goes:
time: 317 us; the launch traced here: 316 us
  waiting for transfers between devices  191 us (60%)
  matrix products  51.1 us (16%)
  blocking collectives  42.7 us (13%)
  between operations  17.9 us (6%)
  local copies, waits for them, and re-layouts  7.55 us (2%)
  other arithmetic  4.11 us (1%)
    reduce_scatter x2, waiting for transfers between devices, section_step(): lax.psum_scatter(jnp.dot(dquery, w_query, preferred_element_type=jnp.floa...  121 us
    all_gather x2, waiting for transfers between devices, section_step(): gathered = lax.all_gather(gradient, 'col', axis=0, tiled=True)  67.4 us
    psum x2, blocking collectives, section_step(): upstream = lax.psum(partial_value, 'row').astype(jnp.bfloat16)  42.7 us
    dot_general x2, matrix products, section_step(): jnp.dot(dquery, w_query, preferred_element_type=jnp.float32)  21.6 us
    dot_general x2, matrix products, section_step(): partial_value = jnp.dot(gathered, w_out, preferred_element_type=jnp.float32)  16.4 us
  transfers between devices with their start and end apart: 5, of which 5 were waited for; matrix products, arithmetic and copies ran while one was open for 4% of the time, Pallas kernels for 0%

commit v1 on v0

v1 whole, which is shorter than its diff:
```python
import functools

import jax
import jax.numpy as jnp
from jax import lax
from jax.experimental import pallas as pl
from jax.experimental.pallas import tpu as pltpu
from jax.sharding import PartitionSpec as P

HD = 128
BLOCK = 64
INVERSE_ROOT = HD ** (-0.5)
F32 = jnp.float32
BF16 = jnp.bfloat16
FIXED = 3
GRANT = 6 << 20
KEPT = 5

HBM = pl.BlockSpec(memory_space=pltpu.HBM)
VMEM = pl.BlockSpec(memory_space=pltpu.VMEM)
SMEM = pl.BlockSpec(memory_space=pltpu.SMEM)


def chunk_of(size, most):
    return max(c for c in range(HD, most + 1, HD) if size % c == 0)


def ring_order(count):
    return list(range(0, count, 2)) + list(range(1, count, 2))[::-1]


def params(limit):
    return pltpu.CompilerParams(vmem_limit_bytes=limit)


def prepare_kernel(heads, copies, pattern_at, facts, wo, wq, sq, sk, sv, wo_v, wq_v, prob, k_sel, v_sel, q_sel, sem):
    turns, tokens, width = q_sel.shape
    pending = []

    def start(source, target):
        copy = pltpu.make_async_copy(source, target, sem.at[len(pending)])
        copy.start()
        pending.append(copy)

    for turn in range(turns):
        for saved, picked in ((sq, q_sel), (sk, k_sel), (sv, v_sel)):
            start(saved.at[facts[1 + turn]], picked.at[turn])
    early = len(pending)
    for weight, held in ((wo, wo_v), (wq, wq_v)):
        rows = weight.shape[0] // copies
        for i in range(copies):
            start(weight.at[pl.ds(i * rows, rows)], held.at[pl.ds(i * rows, rows)])
    for copy in pending[:early]:
        copy.wait()

    blocks = tokens // BLOCK
    listed = (facts.shape[0] - pattern_at) // (heads * blocks)
    row_at = lax.broadcasted_iota(jnp.int32, (tokens, tokens), 0)
    col_at = lax.broadcasted_iota(jnp.int32, (tokens, tokens), 1)

    def one_head(head, carry):
        lanes = pl.ds(pl.multiple_of(head * HD, HD), HD)
        member = jnp.zeros((tokens, tokens), jnp.int32)
        for i in range(blocks):
            for j in range(blocks):
                flag = jnp.int32(0)
                for e in range(listed):
                    entry = facts[pattern_at + (head * blocks + i) * listed + e]
                    flag = jnp.where(entry == j, jnp.int32(1), flag)
                inside = (row_at // BLOCK == i) & (col_at // BLOCK == j)
                member = jnp.where(inside, flag, member)
        allowed = (member > 0) & (col_at <= row_at)
        for turn in range(turns):
            score = (
                lax.dot_general(
                    q_sel[turn, :, lanes],
                    k_sel[turn, :, lanes],
                    (((1,), (1,)), ((), ())),
                    preferred_element_type=F32,
                )
                * INVERSE_ROOT
            )
            masked = jnp.where(allowed, score, -jnp.inf)
            peak = jnp.max(masked, axis=-1, keepdims=True)
            terms = jnp.where(allowed, jnp.exp(masked - peak), 0.0)
            prob[turn, head] = terms / jnp.sum(terms, axis=-1, keepdims=True)
        return carry

    lax.fori_loop(0, heads, one_head, 0)
    for copy in pending[early:]:
        copy.wait()


def prepare(turns, pattern_at, facts, wo, wq, sq, sk, sv):
    tokens, width = sq.shape[1:]
    heads = width // HD
    copies = 8
    return pl.pallas_call(
        functools.partial(prepare_kernel, heads, copies, pattern_at),
        in_specs=[SMEM] + [HBM] * 5,
        out_specs=[VMEM] * 5,
        out_shape=[
            pltpu.VMEM(wo.shape, BF16),
            pltpu.VMEM(wq.shape, BF16),
            pltpu.VMEM((turns, heads, tokens, tokens), F32),
            pltpu.VMEM((turns, tokens, width), BF16),
            pltpu.VMEM((turns, tokens, width), BF16),
        ],
        scratch_shapes=[
            pltpu.VMEM((turns, tokens, width), BF16),
            pltpu.SemaphoreType.DMA((3 * turns + 2 * copies,)),
        ],
        compiler_params=params(GRANT),
        name="prepare",
    )(facts, *(pltpu.with_memory_space_constraint(x, pltpu.HBM) for x in (wo, wq, sq, sk, sv)))


def entry_kernel(count, *refs):
    parts, weight, out = refs[:count], refs[count + 1], refs[count + 1 + KEPT]
    width = weight.shape[1]
    step_width = chunk_of(width, 512)
    if count == 1:
        source = parts[0]
    else:
        source = refs[count + 2 + KEPT]
        rows = parts[0].shape[0]
        for i, part in enumerate(parts):
            source[i * rows : (i + 1) * rows] = part[...]

    def step(i, carry):
        lanes = pl.ds(pl.multiple_of(i * step_width, step_width), step_width)
        out[:, lanes] = jnp.dot(source[...], weight[:, lanes], preferred_element_type=F32).astype(BF16)
        return carry

    lax.fori_loop(0, width // step_width, step, 0)


def entry(parts, facts, kept):
    weight = kept[0]
    rows = parts[0].shape[0] * len(parts)
    scratch = [pltpu.VMEM((rows, weight.shape[0]), BF16)] if len(parts) > 1 else []
    return pl.pallas_call(
        functools.partial(entry_kernel, len(parts)),
        in_specs=[VMEM] * len(parts) + [SMEM] + [VMEM] * KEPT,
        out_specs=VMEM,
        out_shape=pltpu.VMEM((rows, weight.shape[1]), BF16),
        scratch_shapes=scratch,
        compiler_params=params(GRANT),
        name="entry",
    )(*parts, facts, *kept)


def exit_kernel(turn, steps, mine, theirs, facts, _, weight, prob, keys, values, *refs):
    outs, dquery = refs[: len(steps)], refs[len(steps)]
    heads = mine.shape[1] // HD
    rows = mine.shape[0] // len(steps)
    parts = []
    for s, step_at in enumerate(steps):
        here = slice(s * rows, (s + 1) * rows)
        first = pl.multiple_of(facts[FIXED + step_at] * rows, rows)
        for head in range(heads):
            lanes = slice(head * HD, (head + 1) * HD)
            upstream = (mine[here, lanes].astype(F32) + theirs[here, lanes].astype(F32)).astype(BF16)
            prob_grad = lax.dot_general(
                upstream, values[turn, :, lanes], (((1,), (1,)), ((), ())), preferred_element_type=F32
            )
            parts.append((here, lanes, head, first, prob_grad))
    scored = []
    for here, lanes, head, first, prob_grad in parts:
        weights = prob[turn, head, pl.ds(first, rows), :]
        delta = jnp.sum(weights * prob_grad, axis=-1, keepdims=True)
        scored.append((here, lanes, (weights * (prob_grad - delta)).astype(BF16)))
    backs = [
        (here, lanes, jnp.dot(dscore, keys[turn, :, lanes], preferred_element_type=F32))
        for here, lanes, dscore in scored
    ]
    for here, lanes, back in backs:
        dquery[here, lanes] = (back * INVERSE_ROOT).astype(BF16)
    width = weight.shape[1]
    step_width = chunk_of(width, 1024)

    def step(i, carry):
        lanes = pl.ds(pl.multiple_of(i * step_width, step_width), step_width)
        mixed = jnp.dot(dquery[...], weight[:, lanes], preferred_element_type=F32).astype(BF16)
        for s, out in enumerate(outs):
            out[:, lanes] = mixed[s * rows : (s + 1) * rows]
        return carry

    lax.fori_loop(0, width // step_width, step, 0)


def leave(turn, steps, mine, theirs, facts, kept):
    weight = kept[1]
    rows = mine.shape[0] // len(steps)
    return pl.pallas_call(
        functools.partial(exit_kernel, turn, steps),
        in_specs=[VMEM] * 2 + [SMEM] + [VMEM] * KEPT,
        out_specs=[VMEM] * len(steps),
        out_shape=[pltpu.VMEM((rows, weight.shape[1]), BF16)] * len(steps),
        scratch_shapes=[pltpu.VMEM(mine.shape, BF16)],
        compiler_params=params(GRANT),
        name="leave",
    )(mine, theirs, facts, *kept)


def add_kernel(total, part, *refs):
    out = refs[KEPT + 1]
    out[...] = (total[...].astype(F32) + part[...].astype(F32)).astype(BF16)


def add(total, part, facts, kept):
    return pl.pallas_call(
        add_kernel,
        in_specs=[VMEM] * 2 + [SMEM] + [VMEM] * KEPT,
        out_specs=VMEM,
        out_shape=pltpu.VMEM(part.shape, BF16),
        compiler_params=params(GRANT),
        name="add",
    )(total, part, facts, *kept)


def finish_kernel(own, total, part, loss, facts, *refs):
    handed, payload = refs[KEPT:]
    handed[...] = (own[...].astype(F32) + (total[...].astype(F32) + part[...].astype(F32))).astype(BF16)

    @pl.when(facts[0] == 0)
    def _():
        payload[...] = loss[...]

    @pl.when(facts[0] != 0)
    def _():
        payload[...] = handed[...]


def finish(own, total, part, loss, facts, kept):
    return pl.pallas_call(
        finish_kernel,
        in_specs=[VMEM] * 4 + [SMEM] + [VMEM] * KEPT,
        out_specs=[VMEM] * 2,
        out_shape=[jax.ShapeDtypeStruct(own.shape, BF16), pltpu.VMEM(own.shape, BF16)],
        compiler_params=params(GRANT),
        name="finish",
    )(own, total, part, loss, facts, *kept)


def last_kernel(own, total, part, *refs):
    handed = refs[KEPT + 1]
    handed[...] = (own[...].astype(F32) + (total[...].astype(F32) + part[...].astype(F32))).astype(BF16)


def last(own, total, part, facts, kept):
    return pl.pallas_call(
        last_kernel,
        in_specs=[VMEM] * 3 + [SMEM] + [VMEM] * KEPT,
        out_specs=VMEM,
        out_shape=jax.ShapeDtypeStruct(own.shape, BF16),
        compiler_params=params(GRANT),
        name="last",
    )(own, total, part, facts, *kept)


def body(sizes, incoming, loss_grad, out_proj_t, query_proj_t, saved_query, saved_key, saved_value, pattern, plan):
    sections, rows, cols = sizes
    section_at = lax.axis_index("section")
    col_at = lax.axis_index("col")
    order = ring_order(cols)
    after = {order[i]: order[(i + 1) % cols] for i in range(cols)}
    ring = [(c, after[c]) for c in range(cols)]
    before_section = [(s, (s - 1) % sections) for s in range(sections)]
    joint = [
        (s * cols + c, before * cols + after[c]) for s, before in before_section for c in range(cols)
    ]
    place_table = [[order[(order.index(c) - k) % cols] for k in range(cols)] for c in range(cols)]
    place = lax.dynamic_index_in_dim(jnp.array(place_table, jnp.int32), col_at, 0, keepdims=False)
    slots = lax.dynamic_index_in_dim(plan, section_at, 0, keepdims=False)
    heads = out_proj_t.shape[2] // HD
    local_pattern = lax.dynamic_slice_in_dim(pattern, col_at * heads, heads, 0).reshape(-1)
    facts = jnp.concatenate([section_at[None], slots, place, local_pattern])
    turns = plan.shape[1]

    kept = prepare(
        turns, FIXED + cols, facts, out_proj_t[0], query_proj_t[0], saved_query[:, 0], saved_key[:, 0], saved_value[:, 0]
    )

    def from_other_rows(partial):
        moving, total = partial, None
        for _ in range(rows - 1):
            moving = lax.ppermute(moving, "row", [(r, (r + 1) % rows) for r in range(rows)])
            total = moving if total is None else total + moving
        return jnp.zeros_like(partial) if total is None else total

    def turn_of(own, first, turn):
        def contribution(steps, parts):
            partial = entry(parts, facts, kept)
            return leave(turn, steps, partial, from_other_rows(partial), facts, kept)

        moving = first
        later = []
        for k in range(2, cols):
            moving = lax.ppermute(moving, "col", ring)
            later.append((k, moving))
        own_part, total = contribution((0, 1), (own, first))
        total = lax.ppermute(total, "col", ring)
        for k, moved in later:
            (part,) = contribution((k,), (moved,))
            total = lax.ppermute(add(total, part, facts, kept), "col", ring)
        return total, own_part

    own = incoming[0]
    total, part = turn_of(own, lax.ppermute(own, "col", ring), 0)
    handed_first, payload = finish(own, total, part, loss_grad, facts, kept)
    first = lax.ppermute(payload, ("section", "col"), joint)
    second = lax.ppermute(payload, "section", before_section)
    handed_second = last(second, *turn_of(second, first, 1), facts, kept)
    return (handed_first[None], handed_second[None])


def solution(mesh):
    sizes = tuple(mesh.shape[axis] for axis in ("section", "row", "col"))
    return jax.shard_map(
        functools.partial(body, sizes),
        mesh=mesh,
        in_specs=(
            P("section", "col", "row"),
            P("col", "row"),
            P("section", "row", "col"),
            P("section", "col", "row"),
            P(None, "section", None, "col"),
            P(None, "section", None, "col"),
            P(None, "section", None, "col"),
            P(),
            P(),
        ),
        out_specs=(P("section", "col", "row"), P("section", "col", "row")),
        check_vma=False,
    )
```

time: 317 us -> 156 us (0.49)
  waiting for transfers between devices: 191 us -> 42.9 us
  Pallas kernels: 0 us -> 74.1 us
  matrix products: 51.1 us -> 0 us
  blocking collectives: 42.7 us -> 0 us
  starting transfers between devices: 1.45 us -> 36.5 us
  between operations: 17.9 us -> 0.78 us
  local copies, waits for them, and re-layouts: 7.55 us -> 1.86 us
  other arithmetic: 4.11 us -> 0.08 us
    reduce_scatter x2 -> x0, waiting for transfers between devices: 121 us -> none  [section_step(): lax.psum_scatter(jnp.dot(dquery, w_query, preferred_element_type=jnp.floa...]
    pallas_call x0 -> x19, Pallas kernels: none -> 74.1 us  [the longest x6 30.7 us: leave(): pl.pallas_call(functools.partial(exit_kernel, turn, steps), in_specs=[VME...]
    all_gather x2 -> x0, waiting for transfers between devices: 67.4 us -> none  [section_step(): gathered = lax.all_gather(gradient, 'col', axis=0, tiled=True)]
    dot_general x10 -> x0, matrix products: 48.2 us -> none  [the longest x2 21.6 us: section_step(): jnp.dot(dquery, w_query, preferred_element_type=jnp.float32)]
    psum x2 -> x0, blocking collectives: 42.7 us -> none  [section_step(): upstream = lax.psum(partial_value, 'row').astype(jnp.bfloat16)]
    ppermute x1 -> x19, waiting for transfers between devices: 2.31 us -> 42.9 us  [the longest x6 17.5 us: from_other_rows(): lax.ppermute(moving, 'row', [(r, (r + 1) % rows) for r in range(rows)])]
    ppermute x1 -> x19, starting transfers between devices: 1.29 us -> 36.5 us  [the longest x4 9.4 us: turn_of(): total = lax.ppermute(add(total, part, facts, kept), 'col', ring)]
  transfers between devices with their start and end apart: 5 -> 19, of which waited for: 5 -> 12; matrix products, arithmetic and copies ran while one was open for 4% -> 1% of each run, Pallas kernels for 0% -> 39%
where the time goes in v1:
time: 156 us
  Pallas kernels  74.1 us (47%)
  waiting for transfers between devices  42.9 us (28%)
  starting transfers between devices  36.5 us (23%)
  local copies, waits for them, and re-layouts  1.86 us (1%)
    pallas_call x6, Pallas kernels, leave(): pl.pallas_call(functools.partial(exit_kernel, turn, steps), in_specs=[VME...  30.7 us
    pallas_call x6, Pallas kernels, entry(): pl.pallas_call(functools.partial(entry_kernel, len(parts)), in_specs=[VME...  24.8 us
    ppermute x6, waiting for transfers between devices, from_other_rows(): lax.ppermute(moving, 'row', [(r, (r + 1) % rows) for r in range(rows)])  17.5 us
    ppermute x4, waiting for transfers between devices, turn_of(): total = lax.ppermute(add(total, part, facts, kept), 'col', ring)  13.9 us
    pallas_call x1, Pallas kernels, prepare(): pl.pallas_call(functools.partial(prepare_kernel, heads, copies, pattern_a...  13.3 us
    ppermute x4, starting transfers between devices, turn_of(): total = lax.ppermute(add(total, part, facts, kept), 'col', ring)  9.4 us
    ppermute x6, starting transfers between devices, from_other_rows(): lax.ppermute(moving, 'row', [(r, (r + 1) % rows) for r in range(rows)])  9.29 us
    ppermute x4, starting transfers between devices, turn_of(): moving = lax.ppermute(moving, 'col', ring)  6.26 us
  transfers between devices with their start and end apart: 19, of which 12 were waited for; matrix products, arithmetic and copies ran while one was open for 1% of the time, Pallas kernels for 39%

profile of v1, /device:TPU:0, one launch (start us, length us, event | category | flops | bytes accessed | tf_op | source)
XLA Modules:
  0.0 156.2 jit_solution(8966901040499900522)
XLA Ops:
  0.6 4.1 %collective-permute-start = (bf16[32,6144]{1,0:T(8,128)(2,1)}, bf16[32,6144]{1,0:T(8,128)(2,1)S(1)}, u32[]{:S(2)}, u32[]{:S(2)}) collective-permute-start(bf16[32,6144]{1,0:T(8,128)(2,1)} %bitcast.11), channel_id=1, source_target_pairs={{0,2},{1,0},{2,3},{3,1},{4,6},{5,4},{6,7},{7,5},{8,10},{9,8},{10,1... | collective-permute-start | bytes 1179656 | tf_op jit(solution)/shard_map/ppermute | solution.py:310
  6.7 13.3 %prepare.1 = (bf16[6144,1536]{1,0:T(8,128)(2,1)S(1)}, bf16[1536,6144]{1,0:T(8,128)(2,1)S(1)}, f32[2,12,128,128]{3,2,1,0:T(8,128)S(1)}, bf16[2,128,1536]{2,1,0:T(8,128)(2,1)S(1)}, bf16[2,128,1536]{2,1,0:T(8,128)(2,1)S(1)}) custom-call(s32[79]{0:T(128)S(1)} %pad_add_fusion.facts.refs_2_.refs_1_.refs_0_, bf16[6144,1536]{1,0:T(8,128)(2,1)} %bitcast.14, ...), custom_call_target="tpu_custom_call" | custom-call | tf_op jit(solution)/shard_map/prepare/pallas_call | solution.py:98
  20.0 4.3 %entry.6.mine = bf16[64,1536]{1,0:T(8,128)(2,1)S(1)} custom-call(bf16[32,6144]{1,0:T(8,128)(2,1)S(1)} %bitcast.12, bf16[32,6144]{1,0:T(8,128)(2,1)S(1)} %collective-permute-done.refs_1_, s32[79]{0:T(128)S(1)} %pad_add_fusion.facts.refs_2_.refs_1_.refs_0_, bf16[6144,1536]{1,0:T(8,128)(2,1)S(1)} %get-tuple-element.13.refs_3_._.refs_2_.refs_1_.refs_0_, ...), custom_call_target="tpu_custom_call" | custom-call | tf_op jit(solution)/shard_map/entry/pallas_call | solution.py:142
  27.4 3.3 %collective-permute-done.1.theirs = bf16[64,1536]{1,0:T(8,128)(2,1)S(1)} collective-permute-done((bf16[64,1536]{1,0:T(8,128)(2,1)S(1)}, bf16[64,1536]{1,0:T(8,128)(2,1)S(1)}, u32[]{:S(2)}, u32[]{:S(2)}) %collective-permute-start.1) | collective-permute-done | bytes 196640 | tf_op jit(solution)/shard_map/ppermute | solution.py:288
  30.7 5.3 %leave.6 = (bf16[32,6144]{1,0:T(8,128)(2,1)S(1)}, bf16[32,6144]{1,0:T(8,128)(2,1)S(1)}) custom-call(bf16[64,1536]{1,0:T(8,128)(2,1)S(1)} %entry.6.mine, bf16[64,1536]{1,0:T(8,128)(2,1)S(1)} %collective-permute-done.1.theirs, s32[79]{0:T(128)S(1)} %pad_add_fusion.facts.refs_2_.refs_1_.refs_0_, ...), custom_call_target="tpu_custom_call" | custom-call | tf_op jit(solution)/shard_map/leave/pallas_call | solution.py:195
  37.6 4.1 %entry.7.mine = bf16[32,1536]{1,0:T(8,128)(2,1)S(1)} custom-call(bf16[32,6144]{1,0:T(8,128)(2,1)S(1)} %collective-permute-done.3.refs_0_, s32[79]{0:T(128)S(1)} %pad_add_fusion.facts.refs_2_.refs_1_.refs_0_, bf16[6144,1536]{1,0:T(8,128)(2,1)S(1)} %get-tuple-element.13.refs_3_._.refs_2_.refs_1_.refs_0_, ...), custom_call_target="tpu_custom_call" | custom-call | tf_op jit(solution)/shard_map/entry/pallas_call | solution.py:142
  46.3 5.0 %leave.7.part = bf16[32,6144]{1,0:T(8,128)(2,1)S(1)} custom-call(bf16[32,1536]{1,0:T(8,128)(2,1)S(1)} %entry.7.mine, bf16[32,1536]{1,0:T(8,128)(2,1)S(1)} %collective-permute-done.4.theirs, s32[79]{0:T(128)S(1)} %pad_add_fusion.facts.refs_2_.refs_1_.refs_0_, bf16[6144,1536]{1,0:T(8,128)(2,1)S(1)} %get-tuple-element.13.refs_3_._.refs_2_.refs_1_.refs_0_, ...), custom_call_target="tpu_custom_call" | custom-call | tf_op jit(solution)/shard_map/leave/pallas_call | solution.py:195
  53.0 3.0 %collective-permute-done.6.refs_0_ = bf16[32,6144]{1,0:T(8,128)(2,1)S(1)} collective-permute-done((bf16[32,6144]{1,0:T(8,128)(2,1)S(1)}, bf16[32,6144]{1,0:T(8,128)(2,1)S(1)}, u32[]{:S(2)}, u32[]{:S(2)}) %collective-permute-start.6) | collective-permute-done | bytes 393248 | tf_op jit(solution)/shard_map/ppermute | solution.py:300
  56.0 4.1 %entry.8.mine = bf16[32,1536]{1,0:T(8,128)(2,1)S(1)} custom-call(bf16[32,6144]{1,0:T(8,128)(2,1)S(1)} %collective-permute-done.6.refs_0_, s32[79]{0:T(128)S(1)} %pad_add_fusion.facts.refs_2_.refs_1_.refs_0_, bf16[6144,1536]{1,0:T(8,128)(2,1)S(1)} %get-tuple-element.13.refs_3_._.refs_2_.refs_1_.refs_0_, ...), custom_call_target="tpu_custom_call" | custom-call | tf_op jit(solution)/shard_map/entry/pallas_call | solution.py:142
  61.8 3.0 %collective-permute-done.7.theirs = bf16[32,1536]{1,0:T(8,128)(2,1)S(1)} collective-permute-done((bf16[32,1536]{1,0:T(8,128)(2,1)S(1)}, bf16[32,1536]{1,0:T(8,128)(2,1)S(1)}, u32[]{:S(2)}, u32[]{:S(2)}) %collective-permute-start.7) | collective-permute-done | bytes 98336 | tf_op jit(solution)/shard_map/ppermute | solution.py:288
  64.7 5.0 %leave.8.part = bf16[32,6144]{1,0:T(8,128)(2,1)S(1)} custom-call(bf16[32,1536]{1,0:T(8,128)(2,1)S(1)} %entry.8.mine, bf16[32,1536]{1,0:T(8,128)(2,1)S(1)} %collective-permute-done.7.theirs, s32[79]{0:T(128)S(1)} %pad_add_fusion.facts.refs_2_.refs_1_.refs_0_, bf16[6144,1536]{1,0:T(8,128)(2,1)S(1)} %get-tuple-element.13.refs_3_._.refs_2_.refs_1_.refs_0_, ...), custom_call_target="tpu_custom_call" | custom-call | tf_op jit(solution)/shard_map/leave/pallas_call | solution.py:195
  73.3 5.3 %collective-permute-done.8.total = bf16[32,6144]{1,0:T(8,128)(2,1)S(1)} collective-permute-done((bf16[32,6144]{1,0:T(8,128)(2,1)S(1)}, bf16[32,6144]{1,0:T(8,128)(2,1)S(1)}, u32[]{:S(2)}, u32[]{:S(2)}) %collective-permute-start.8) | collective-permute-done | bytes 393248 | tf_op jit(solution)/shard_map/ppermute | solution.py:306
  80.1 4.5 %collective-permute-start.10 = (bf16[32,6144]{1,0:T(8,128)(2,1)S(1)}, bf16[32,6144]{1,0:T(8,128)(2,1)S(1)}, u32[]{:S(2)}, u32[]{:S(2)}) collective-permute-start(bf16[32,6144]{1,0:T(8,128)(2,1)S(1)} %get-tuple-element.21), channel_id=1, source_target_pairs={{0,26},{1,24},{2,27},{3,25},{8,2},{9,0},{10,3},{11,1},{16,10},{17,... | collective-permute-start | bytes 1179656 | tf_op jit(solution)/shard_map/ppermute | solution.py:312
  86.9 5.5 %collective-permute-done.10.refs_1_ = bf16[32,6144]{1,0:T(8,128)(2,1)S(1)} collective-permute-done((bf16[32,6144]{1,0:T(8,128)(2,1)S(1)}, bf16[32,6144]{1,0:T(8,128)(2,1)S(1)}, u32[]{:S(2)}, u32[]{:S(2)}) %collective-permute-start.10) | collective-permute-done | bytes 393248 | tf_op jit(solution)/shard_map/ppermute | solution.py:312
  92.4 4.3 %entry.9.mine = bf16[64,1536]{1,0:T(8,128)(2,1)S(1)} custom-call(bf16[32,6144]{1,0:T(8,128)(2,1)S(1)} %collective-permute-done.9.refs_0_.own, bf16[32,6144]{1,0:T(8,128)(2,1)S(1)} %collective-permute-done.10.refs_1_, s32[79]{0:T(128)S(1)} %pad_add_fusion.facts.refs_2_.refs_1_.refs_0_, ...), custom_call_target="tpu_custom_call" | custom-call | tf_op jit(solution)/shard_map/entry/pallas_call | solution.py:142
  100.0 3.4 %collective-permute-done.11.theirs = bf16[64,1536]{1,0:T(8,128)(2,1)S(1)} collective-permute-done((bf16[64,1536]{1,0:T(8,128)(2,1)S(1)}, bf16[64,1536]{1,0:T(8,128)(2,1)S(1)}, u32[]{:S(2)}, u32[]{:S(2)}) %collective-permute-start.11) | collective-permute-done | bytes 196640 | tf_op jit(solution)/shard_map/ppermute | solution.py:288
  103.5 5.3 %leave.9 = (bf16[32,6144]{1,0:T(8,128)(2,1)S(1)}, bf16[32,6144]{1,0:T(8,128)(2,1)S(1)}) custom-call(bf16[64,1536]{1,0:T(8,128)(2,1)S(1)} %entry.9.mine, bf16[64,1536]{1,0:T(8,128)(2,1)S(1)} %collective-permute-done.11.theirs, s32[79]{0:T(128)S(1)} %pad_add_fusion.facts.refs_2_.refs_1_.refs_0_, ...), custom_call_target="tpu_custom_call" | custom-call | tf_op jit(solution)/shard_map/leave/pallas_call | solution.py:195
  110.1 4.1 %entry.10.mine = bf16[32,1536]{1,0:T(8,128)(2,1)S(1)} custom-call(bf16[32,6144]{1,0:T(8,128)(2,1)S(1)} %collective-permute-done.13.refs_0_, s32[79]{0:T(128)S(1)} %pad_add_fusion.facts.refs_2_.refs_1_.refs_0_, bf16[6144,1536]{1,0:T(8,128)(2,1)S(1)} %get-tuple-element.13.refs_3_._.refs_2_.refs_1_.refs_0_, ...), custom_call_target="tpu_custom_call" | custom-call | tf_op jit(solution)/shard_map/entry/pallas_call | solution.py:142
  119.5 5.0 %leave.10.part = bf16[32,6144]{1,0:T(8,128)(2,1)S(1)} custom-call(bf16[32,1536]{1,0:T(8,128)(2,1)S(1)} %entry.10.mine, bf16[32,1536]{1,0:T(8,128)(2,1)S(1)} %collective-permute-done.14.theirs, s32[79]{0:T(128)S(1)} %pad_add_fusion.facts.refs_2_.refs_1_.refs_0_, bf16[6144,1536]{1,0:T(8,128)(2,1)S(1)} %get-tuple-element.13.refs_3_._.refs_2_.refs_1_.refs_0_, ...), custom_call_target="tpu_custom_call" | custom-call | tf_op jit(solution)/shard_map/leave/pallas_call | solution.py:195
  127.8 4.1 %entry.11.mine = bf16[32,1536]{1,0:T(8,128)(2,1)S(1)} custom-call(bf16[32,6144]{1,0:T(8,128)(2,1)S(1)} %collective-permute-done.16.refs_0_, s32[79]{0:T(128)S(1)} %pad_add_fusion.facts.refs_2_.refs_1_.refs_0_, bf16[6144,1536]{1,0:T(8,128)(2,1)S(1)} %get-tuple-element.13.refs_3_._.refs_2_.refs_1_.refs_0_, ...), custom_call_target="tpu_custom_call" | custom-call | tf_op jit(solution)/shard_map/entry/pallas_call | solution.py:142
  133.2 4.0 %collective-permute-done.17.theirs = bf16[32,1536]{1,0:T(8,128)(2,1)S(1)} collective-permute-done((bf16[32,1536]{1,0:T(8,128)(2,1)S(1)}, bf16[32,1536]{1,0:T(8,128)(2,1)S(1)}, u32[]{:S(2)}, u32[]{:S(2)}) %collective-permute-start.17) | collective-permute-done | bytes 98336 | tf_op jit(solution)/shard_map/ppermute | solution.py:288
  137.1 5.0 %leave.11.part = bf16[32,6144]{1,0:T(8,128)(2,1)S(1)} custom-call(bf16[32,1536]{1,0:T(8,128)(2,1)S(1)} %entry.11.mine, bf16[32,1536]{1,0:T(8,128)(2,1)S(1)} %collective-permute-done.17.theirs, s32[79]{0:T(128)S(1)} %pad_add_fusion.facts.refs_2_.refs_1_.refs_0_, bf16[6144,1536]{1,0:T(8,128)(2,1)S(1)} %get-tuple-element.13.refs_3_._.refs_2_.refs_1_.refs_0_, ...), custom_call_target="tpu_custom_call" | custom-call | tf_op jit(solution)/shard_map/leave/pallas_call | solution.py:195
  142.8 3.4 %collective-permute-start.18 = (bf16[32,6144]{1,0:T(8,128)(2,1)S(1)}, bf16[32,6144]{1,0:T(8,128)(2,1)S(1)}, u32[]{:S(2)}, u32[]{:S(2)}) collective-permute-start(bf16[32,6144]{1,0:T(8,128)(2,1)S(1)} %add.28), channel_id=1, source_target_pairs={{0,2},{1,0},{2,3},{3,1},{4,6},{5,4},{6,7},{7,5},{8,10},{9,8},{10,1... | collective-permute-start | bytes 1179656 | tf_op jit(solution)/shard_map/ppermute | solution.py:306
  146.2 8.6 %collective-permute-done.18.total = bf16[32,6144]{1,0:T(8,128)(2,1)S(1)} collective-permute-done((bf16[32,6144]{1,0:T(8,128)(2,1)S(1)}, bf16[32,6144]{1,0:T(8,128)(2,1)S(1)}, u32[]{:S(2)}, u32[]{:S(2)}) %collective-permute-start.18) | collective-permute-done | bytes 393248 | tf_op jit(solution)/shard_map/ppermute | solution.py:306
  (47 shorter events, 38.6 us)
Async XLA Ops:
  0.6 4.1 %copy-start = (s32[48,2,3]{0,1,2:T(2,128)S(1)}, s32[48,2,3]{0,1,2:T(2,128)}, u32[]{:S(2)}) copy-start(s32[48,2,3]{0,1,2:T(2,128)} %param.17) | copy-start | bytes 3460
  0.6 19.3 %collective-permute-start = (bf16[32,6144]{1,0:T(8,128)(2,1)}, bf16[32,6144]{1,0:T(8,128)(2,1)S(1)}, u32[]{:S(2)}, u32[]{:S(2)}) collective-permute-start(bf16[32,6144]{1,0:T(8,128)(2,1)} %bitcast.11), channel_id=1, source_target_pairs={{0,2},{1,0},{2,3},{3,1},{4,6},{5,4},{6,7},{7,5},{8,10},{9,8},{10,1... | collective-permute-start | bytes 1179656 | tf_op jit(solution)/shard_map/ppermute | solution.py:310
  6.7 13.3 %copy-start.2 = (bf16[1,32,6144]{2,1,0:T(8,128)(2,1)S(1)}, bf16[1,32,6144]{2,1,0:T(8,128)(2,1)}, u32[]{:S(2)}) copy-start(bf16[1,32,6144]{2,1,0:T(8,128)(2,1)} %param.10) | copy-start | bytes 1179652
  24.2 6.4 %collective-permute-start.1 = (bf16[64,1536]{1,0:T(8,128)(2,1)S(1)}, bf16[64,1536]{1,0:T(8,128)(2,1)S(1)}, u32[]{:S(2)}, u32[]{:S(2)}) collective-permute-start(bf16[64,1536]{1,0:T(8,128)(2,1)S(1)} %entry.6.mine), channel_id=1, source_target_pairs={{0,4},{4,0},{1,5},{5,1},{2,6},{6,2},{3,7},{7,3},{8,12},{12,8},{9,1... | collective-permute-start | bytes 589832 | tf_op jit(solution)/shard_map/ppermute | solution.py:288
  25.8 11.8 %collective-permute-start.3 = (bf16[32,6144]{1,0:T(8,128)(2,1)S(1)}, bf16[32,6144]{1,0:T(8,128)(2,1)S(1)}, u32[]{:S(2)}, u32[]{:S(2)}) collective-permute-start(bf16[32,6144]{1,0:T(8,128)(2,1)S(1)} %collective-permute-done.refs_1_), channel_id=1, source_target_pairs={{0,2},{1,0},{2,3},{3,1},{4,6},{5,4},{6,7},{7,5},{8,10},{9,8},{10,1... | collective-permute-start | bytes 1179656 | tf_op jit(solution)/shard_map/ppermute | solution.py:300
  36.0 15.3 %collective-permute-start.2 = (bf16[32,6144]{1,0:T(8,128)(2,1)S(1)}, bf16[32,6144]{1,0:T(8,128)(2,1)S(1)}, u32[]{:S(2)}, u32[]{:S(2)}) collective-permute-start(bf16[32,6144]{1,0:T(8,128)(2,1)S(1)} %get-tuple-element.18), channel_id=1, source_target_pairs={{0,2},{1,0},{2,3},{3,1},{4,6},{5,4},{6,7},{7,5},{8,10},{9,8},{10,1... | collective-permute-start | bytes 1179656 | tf_op jit(solution)/shard_map/ppermute | solution.py:303
  41.7 4.6 %collective-permute-start.4 = (bf16[32,1536]{1,0:T(8,128)(2,1)S(1)}, bf16[32,1536]{1,0:T(8,128)(2,1)S(1)}, u32[]{:S(2)}, u32[]{:S(2)}) collective-permute-start(bf16[32,1536]{1,0:T(8,128)(2,1)S(1)} %entry.7.mine), channel_id=1, source_target_pairs={{0,4},{4,0},{1,5},{5,1},{2,6},{6,2},{3,7},{7,3},{8,12},{12,8},{9,1... | collective-permute-start | bytes 294920 | tf_op jit(solution)/shard_map/ppermute | solution.py:288
  43.2 12.8 %collective-permute-start.6 = (bf16[32,6144]{1,0:T(8,128)(2,1)S(1)}, bf16[32,6144]{1,0:T(8,128)(2,1)S(1)}, u32[]{:S(2)}, u32[]{:S(2)}) collective-permute-start(bf16[32,6144]{1,0:T(8,128)(2,1)S(1)} %collective-permute-done.3.refs_0_), channel_id=1, source_target_pairs={{0,2},{1,0},{2,3},{3,1},{4,6},{5,4},{6,7},{7,5},{8,10},{9,8},{10,1... | collective-permute-start | bytes 1179656 | tf_op jit(solution)/shard_map/ppermute | solution.py:300
  52.0 17.7 %collective-permute-start.5 = (bf16[32,6144]{1,0:T(8,128)(2,1)S(1)}, bf16[32,6144]{1,0:T(8,128)(2,1)S(1)}, u32[]{:S(2)}, u32[]{:S(2)}) collective-permute-start(bf16[32,6144]{1,0:T(8,128)(2,1)S(1)} %add.25), channel_id=1, source_target_pairs={{0,2},{1,0},{2,3},{3,1},{4,6},{5,4},{6,7},{7,5},{8,10},{9,8},{10,1... | collective-permute-start | bytes 1179656 | tf_op jit(solution)/shard_map/ppermute | solution.py:306
  60.1 4.6 %collective-permute-start.7 = (bf16[32,1536]{1,0:T(8,128)(2,1)S(1)}, bf16[32,1536]{1,0:T(8,128)(2,1)S(1)}, u32[]{:S(2)}, u32[]{:S(2)}) collective-permute-start(bf16[32,1536]{1,0:T(8,128)(2,1)S(1)} %entry.8.mine), channel_id=1, source_target_pairs={{0,4},{4,0},{1,5},{5,1},{2,6},{6,2},{3,7},{7,3},{8,12},{12,8},{9,1... | collective-permute-start | bytes 294920 | tf_op jit(solution)/shard_map/ppermute | solution.py:288
  69.7 8.9 %copy-start.3 = (bf16[32,6144]{1,0:T(8,128)(2,1)S(1)}, bf16[32,6144]{1,0:T(8,128)(2,1)}, u32[]{:S(2)}) copy-start(bf16[32,6144]{1,0:T(8,128)(2,1)} %loss.1) | copy-start | bytes 1179652
  70.4 8.2 %collective-permute-start.8 = (bf16[32,6144]{1,0:T(8,128)(2,1)S(1)}, bf16[32,6144]{1,0:T(8,128)(2,1)S(1)}, u32[]{:S(2)}, u32[]{:S(2)}) collective-permute-start(bf16[32,6144]{1,0:T(8,128)(2,1)S(1)} %add.26), channel_id=1, source_target_pairs={{0,2},{1,0},{2,3},{3,1},{4,6},{5,4},{6,7},{7,5},{8,10},{9,8},{10,1... | collective-permute-start | bytes 1179656 | tf_op jit(solution)/shard_map/ppermute | solution.py:306
  80.1 6.8 %collective-permute-start.9 = (bf16[32,6144]{1,0:T(8,128)(2,1)S(1)}, bf16[32,6144]{1,0:T(8,128)(2,1)S(1)}, u32[]{:S(2)}, u32[]{:S(2)}) collective-permute-start(bf16[32,6144]{1,0:T(8,128)(2,1)S(1)} %get-tuple-element.21), channel_id=1, source_target_pairs={{0,24},{8,0},{16,8},{24,16},{1,25},{9,1},{17,9},{25,17},{2,26},{10... | collective-permute-start | bytes 1179656 | tf_op jit(solution)/shard_map/ppermute | solution.py:313
  80.1 12.3 %collective-permute-start.10 = (bf16[32,6144]{1,0:T(8,128)(2,1)S(1)}, bf16[32,6144]{1,0:T(8,128)(2,1)S(1)}, u32[]{:S(2)}, u32[]{:S(2)}) collective-permute-start(bf16[32,6144]{1,0:T(8,128)(2,1)S(1)} %get-tuple-element.21), channel_id=1, source_target_pairs={{0,26},{1,24},{2,27},{3,25},{8,2},{9,0},{10,3},{11,1},{16,10},{17,... | collective-permute-start | bytes 1179656 | tf_op jit(solution)/shard_map/ppermute | solution.py:312
  96.7 6.8 %collective-permute-start.11 = (bf16[64,1536]{1,0:T(8,128)(2,1)S(1)}, bf16[64,1536]{1,0:T(8,128)(2,1)S(1)}, u32[]{:S(2)}, u32[]{:S(2)}) collective-permute-start(bf16[64,1536]{1,0:T(8,128)(2,1)S(1)} %entry.9.mine), channel_id=1, source_target_pairs={{0,4},{4,0},{1,5},{5,1},{2,6},{6,2},{3,7},{7,3},{8,12},{12,8},{9,1... | collective-permute-start | bytes 589832 | tf_op jit(solution)/shard_map/ppermute | solution.py:288
  98.3 11.8 %collective-permute-start.13 = (bf16[32,6144]{1,0:T(8,128)(2,1)S(1)}, bf16[32,6144]{1,0:T(8,128)(2,1)S(1)}, u32[]{:S(2)}, u32[]{:S(2)}) collective-permute-start(bf16[32,6144]{1,0:T(8,128)(2,1)S(1)} %collective-permute-done.10.refs_1_), channel_id=1, source_target_pairs={{0,2},{1,0},{2,3},{3,1},{4,6},{5,4},{6,7},{7,5},{8,10},{9,8},{10,1... | collective-permute-start | bytes 1179656 | tf_op jit(solution)/shard_map/ppermute | solution.py:300
  108.8 15.7 %collective-permute-start.12 = (bf16[32,6144]{1,0:T(8,128)(2,1)S(1)}, bf16[32,6144]{1,0:T(8,128)(2,1)S(1)}, u32[]{:S(2)}, u32[]{:S(2)}) collective-permute-start(bf16[32,6144]{1,0:T(8,128)(2,1)S(1)} %get-tuple-element.22), channel_id=1, source_target_pairs={{0,2},{1,0},{2,3},{3,1},{4,6},{5,4},{6,7},{7,5},{8,10},{9,8},{10,1... | collective-permute-start | bytes 1179656 | tf_op jit(solution)/shard_map/ppermute | solution.py:303
  114.2 5.3 %collective-permute-start.14 = (bf16[32,1536]{1,0:T(8,128)(2,1)S(1)}, bf16[32,1536]{1,0:T(8,128)(2,1)S(1)}, u32[]{:S(2)}, u32[]{:S(2)}) collective-permute-start(bf16[32,1536]{1,0:T(8,128)(2,1)S(1)} %entry.10.mine), channel_id=1, source_target_pairs={{0,4},{4,0},{1,5},{5,1},{2,6},{6,2},{3,7},{7,3},{8,12},{12,8},{9,1... | collective-permute-start | bytes 294920 | tf_op jit(solution)/shard_map/ppermute | solution.py:288
  115.8 11.9 %collective-permute-start.16 = (bf16[32,6144]{1,0:T(8,128)(2,1)S(1)}, bf16[32,6144]{1,0:T(8,128)(2,1)S(1)}, u32[]{:S(2)}, u32[]{:S(2)}) collective-permute-start(bf16[32,6144]{1,0:T(8,128)(2,1)S(1)} %collective-permute-done.13.refs_0_), channel_id=1, source_target_pairs={{0,2},{1,0},{2,3},{3,1},{4,6},{5,4},{6,7},{7,5},{8,10},{9,8},{10,1... | collective-permute-start | bytes 1179656 | tf_op jit(solution)/shard_map/ppermute | solution.py:300
  125.2 17.0 %collective-permute-start.15 = (bf16[32,6144]{1,0:T(8,128)(2,1)S(1)}, bf16[32,6144]{1,0:T(8,128)(2,1)S(1)}, u32[]{:S(2)}, u32[]{:S(2)}) collective-permute-start(bf16[32,6144]{1,0:T(8,128)(2,1)S(1)} %add.27), channel_id=1, source_target_pairs={{0,2},{1,0},{2,3},{3,1},{4,6},{5,4},{6,7},{7,5},{8,10},{9,8},{10,1... | collective-permute-start | bytes 1179656 | tf_op jit(solution)/shard_map/ppermute | solution.py:306
  131.8 5.3 %collective-permute-start.17 = (bf16[32,1536]{1,0:T(8,128)(2,1)S(1)}, bf16[32,1536]{1,0:T(8,128)(2,1)S(1)}, u32[]{:S(2)}, u32[]{:S(2)}) collective-permute-start(bf16[32,1536]{1,0:T(8,128)(2,1)S(1)} %entry.11.mine), channel_id=1, source_target_pairs={{0,4},{4,0},{1,5},{5,1},{2,6},{6,2},{3,7},{7,3},{8,12},{12,8},{9,1... | collective-permute-start | bytes 294920 | tf_op jit(solution)/shard_map/ppermute | solution.py:288
  142.8 12.0 %collective-permute-start.18 = (bf16[32,6144]{1,0:T(8,128)(2,1)S(1)}, bf16[32,6144]{1,0:T(8,128)(2,1)S(1)}, u32[]{:S(2)}, u32[]{:S(2)}) collective-permute-start(bf16[32,6144]{1,0:T(8,128)(2,1)S(1)} %add.28), channel_id=1, source_target_pairs={{0,2},{1,0},{2,3},{3,1},{4,6},{5,4},{6,7},{7,5},{8,10},{9,8},{10,1... | collective-permute-start | bytes 1179656 | tf_op jit(solution)/shard_map/ppermute | solution.py:306
  154.8 1.4 copy-start.1
